TPU v7x, 256 devices: a whole 4x4x8 slice. The times are simulated.
256 devices in a mesh: tm: 4 (over y), space: 64 (over x, z, core).
Axes of the slice: x: 4, y: 4, z: 8, core: 2. Of those that a mesh axis runs over, the one named last changes fastest.
Arguments:
- queries: bfloat16 [16, 4096, 1536], P('tm', 'space'), may hold values from -48 to 48
- key_rows: bfloat16 [16, 4096, 1536], P('tm', 'space'), may hold values from -4 to 4
- value_rows: bfloat16 [16, 4096, 1536], P('tm', 'space'), may hold values from -6 to 6
- dropout: int32 [4, 16, 4096, 12], P(None, 'tm', 'space'), may hold values 0 or 1
- tile_lists: int32 [64, 2], P('space'), may hold values from 0 to 63, as said below
Outputs:
- sampled_heads: bfloat16 [4, 16, 4096, 1536], P(None, 'tm', 'space')
Inputs may be any that keep to these rules, and one draw needn't show every extreme that they name: `tile_lists`: row t holds t first and then (t - 1) or (t + 1) modulo 64.
All inputs are finite; a program needn't handle non-finite values. No bound on the sum of `dropout` on one device may be relied on, other than what follows from the above.
Results may differ from a plain program's by a relative error of at most 0.0045.
Values may be sent and summed in bfloat16 or wider, within the bound.
No kernel may reach another device: no remote copies, remote signals or barrier semaphores. Data moves between devices by JAX's collectives and lax.ppermute only.
A program may use at most 128 MiB of HBM per device.

v0:
```python
import math
import jax
import jax.numpy as jnp
from jax import lax
from jax.sharding import PartitionSpec as P

keep_rate = 0.9


def from_behind(shard, axis, by):
    peers = lax.axis_size(axis)
    return lax.ppermute(shard, axis, [(i, (i + by) % peers) for i in range(peers)])


def per_device(queries, key_rows, value_rows, dropout, tile_lists):
    frame_dev, tile_tok, width = queries.shape
    samples = dropout.shape[0]
    head_count = dropout.shape[3]
    head_dim = width // head_count
    factor = 1.0 / math.sqrt(head_dim)
    space_size = lax.axis_size("space")
    tile_here = lax.axis_index("space")
    span_here = lax.axis_index("tm")
    listed = tile_lists[0]
    drop_low = dropout.astype(jnp.bfloat16)
    all_keys, all_values, all_drops = (
        lax.all_gather(key_rows, "tm", axis=0, tiled=True),
        lax.all_gather(value_rows, "tm", axis=0, tiled=True),
        lax.all_gather(drop_low, "tm", axis=1, tiled=True),
    )
    key_parts = [all_keys]
    value_parts = [all_values]
    drop_parts = [all_drops]
    tile_ids = [tile_here]
    for offset in (1, -1):
        moved_keys, moved_values, moved_drops = from_behind(
            (all_keys, all_values, all_drops), "space", offset
        )
        key_parts.append(moved_keys)
        value_parts.append(moved_values)
        drop_parts.append(moved_drops)
        tile_ids.append((tile_here - offset) % space_size)
    window_keys = jnp.stack(key_parts, axis=1)
    window_values = jnp.stack(value_parts, axis=1)
    window_drops = jnp.stack(drop_parts, axis=2)
    tile_valid = jnp.stack([jnp.any(listed == ident) for ident in tile_ids])
    frames_all = window_keys.shape[0]
    window_count = window_keys.shape[1]
    key_total = frames_all * window_count * tile_tok
    key_flat = window_keys.reshape(key_total, width)
    value_flat = window_values.reshape(key_total, width)
    drop_heads = window_drops.reshape(samples, key_total, head_count).transpose(2, 0, 1)
    key_frame = jnp.repeat(jnp.arange(frames_all, dtype=jnp.int32), window_count * tile_tok)
    key_valid = jnp.tile(jnp.repeat(tile_valid, tile_tok), frames_all)
    query_frame = span_here * frame_dev + jnp.repeat(
        jnp.arange(frame_dev, dtype=jnp.int32), tile_tok
    )
    query_block = queries.reshape(frame_dev * tile_tok, width)
    key_limit = frames_all * window_count * tile_tok
    row_count = query_block.shape[0]
    allowed = (key_frame[None, :key_limit] <= query_frame[:, None]) & key_valid[None, :key_limit]

    def one_head(head, output):
        start = head * head_dim
        query_h = lax.dynamic_slice_in_dim(query_block, start, head_dim, 1)
        key_h = lax.dynamic_slice_in_dim(key_flat, start, head_dim, 1)
        value_h = lax.dynamic_slice_in_dim(value_flat, start, head_dim, 1)
        drop_h = lax.dynamic_index_in_dim(drop_heads, head, 0, keepdims=False)
        scores = (
            jnp.einsum("rd,kd->rk", query_h, key_h, preferred_element_type=jnp.float32) * factor
        )
        masked = jnp.where(allowed, scores, -1e30)
        highest = jnp.max(masked, axis=1, keepdims=True)
        weight = jnp.exp(masked - highest)
        total = jnp.sum(weight, axis=1)
        weight_low = weight.astype(jnp.bfloat16)
        dropped = weight_low[None] * drop_h[:, None, :]
        summed = jnp.einsum("srk,kd->srd", dropped, value_h, preferred_element_type=jnp.float32)
        result = (summed / (keep_rate * total)[None, :, None]).astype(jnp.bfloat16)
        return lax.dynamic_update_slice_in_dim(output, result, start, 2)

    initial = jnp.zeros((samples, row_count, width), jnp.bfloat16)
    output = lax.fori_loop(0, head_count, one_head, initial)
    return output.reshape(samples, frame_dev, tile_tok, width)


def solution(mesh):
    placed = (
        P("tm", "space", None),
        P("tm", "space", None),
        P("tm", "space", None),
        P(None, "tm", "space", None),
        P("space", None),
    )
    return jax.shard_map(
        per_device,
        mesh=mesh,
        in_specs=placed,
        out_specs=P(None, "tm", "space", None),
        check_vma=False,
    )
```

profile of v0, /device:TPU:97, one launch (start us, length us, event | category | flops | bytes accessed | tf_op | source)
XLA Modules:
  0.0 245.5 jit_solution(12780342836422055700)
XLA Ops:
  6.5 0.7 all-gather.5.cloned.1.call-update
  7.3 0.7 all-gather.3.cloned.1.call-update
  8.0 44.9 %all-gather.5.cloned.1.call-done = bf16[16,64,1536]{2,1,0:T(8,128)(2,1)} async-done(((bf16[4,64,1536]{2,1,0:T(8,128)(2,1)}), bf16[16,64,1536]{2,1,0:T(8,128)(2,1)}) %all-gather.5.cloned.1.call-update) | async-done | bytes 3145744 | tf_op jit(solution)/shard_map/all_gather | solution.py:28
  52.9 3.2 %collective-permute-start.4 = (bf16[16,64,1536]{2,1,0:T(8,128)(2,1)}, bf16[16,64,1536]{2,1,0:T(8,128)(2,1)S(1)}, u32[]{:S(2)}, u32[]{:S(2)}) collective-permute-start(bf16[16,64,1536]{2,1,0:T(8,128)(2,1)} %all-gather.5.cloned.1.call-done), channel_id=1, source_target_pairs={{0,1},{1,2},{2,3},{3,4},{4,5},{5,6},{6,7},{7,8},{8,9},{9,10},{10,1... | collective-permute-start | bytes 9437192 | tf_op jit(solution)/shard_map/ppermute | solution.py:12
  56.2 40.9 %all-gather.3.cloned.1.call-done = bf16[16,64,1536]{2,1,0:T(8,128)(2,1)} async-done(((bf16[4,64,1536]{2,1,0:T(8,128)(2,1)}), bf16[16,64,1536]{2,1,0:T(8,128)(2,1)}) %all-gather.3.cloned.1.call-update) | async-done | bytes 3145744 | tf_op jit(solution)/shard_map/all_gather | solution.py:27
  97.0 3.2 %collective-permute-start = (bf16[16,64,1536]{2,1,0:T(8,128)(2,1)}, bf16[16,64,1536]{2,1,0:T(8,128)(2,1)}, u32[]{:S(2)}, u32[]{:S(2)}) collective-permute-start(bf16[16,64,1536]{2,1,0:T(8,128)(2,1)} %all-gather.3.cloned.1.call-done), channel_id=1, source_target_pairs={{0,1},{1,2},{2,3},{3,4},{4,5},{5,6},{6,7},{7,8},{8,9},{9,10},{10,1... | collective-permute-start | bytes 9437192 | tf_op jit(solution)/shard_map/ppermute | solution.py:12
  100.3 0.9 copy_convert_fusion
  101.2 9.6 %all_gather.10 = bf16[4,16,64,12]{2,0,3,1:T(4,128)(2,1)S(1)} all-gather(bf16[4,4,64,12]{2,0,3,1:T(4,128)(2,1)S(1)} %copy_convert_fusion), channel_id=1, replica_groups=mesh['tm'=4,'space'=64] {'tm'}, dimensions={1}, use_global_device_ids=true | all-gather | bytes 122880 | tf_op jit(solution)/shard_map/all_gather | solution.py:29
  110.8 5.5 %collective-permute-start.2 = (bf16[4,16,64,12]{2,0,3,1:T(4,128)(2,1)S(1)}, bf16[4,16,64,12]{2,0,3,1:T(4,128)(2,1)S(1)}, u32[]{:S(2)}, u32[]{:S(2)}) collective-permute-start(bf16[4,16,64,12]{2,0,3,1:T(4,128)(2,1)S(1)} %all_gather.10), channel_id=1, source_target_pairs={{0,1},{1,2},{2,3},{3,4},{4,5},{5,6},{6,7},{7,8},{8,9},{9,10},{10,1... | collective-permute-start | bytes 294920 | tf_op jit(solution)/shard_map/ppermute | solution.py:12
  116.3 1.4 compare_reduce_fusion.2
  117.7 2.0 pad_add_fusion
  119.9 0.7 and.23
  120.6 16.2 %collective-permute-done.2 = bf16[4,16,64,12]{2,0,3,1:T(4,128)(2,1)S(1)} collective-permute-done((bf16[4,16,64,12]{2,0,3,1:T(4,128)(2,1)S(1)}, bf16[4,16,64,12]{2,0,3,1:T(4,128)(2,1)S(1)}, u32[]{:S(2)}, u32[]{:S(2)}) %collective-permute-start.2) | collective-permute-done | bytes 98336 | tf_op jit(solution)/shard_map/ppermute | solution.py:12
  136.9 0.7 add.56
  137.6 0.7 le.15
  138.2 5.7 %collective-permute-done.3 = bf16[4,16,64,12]{2,0,3,1:T(4,128)(2,1)} collective-permute-done((bf16[4,16,64,12]{2,0,3,1:T(4,128)(2,1)S(1)}, bf16[4,16,64,12]{2,0,3,1:T(4,128)(2,1)}, u32[]{:S(2)}, u32[]{:S(2)}) %collective-permute-start.3) | collective-permute-done | bytes 98336 | tf_op jit(solution)/shard_map/ppermute | solution.py:12
  143.9 1.5 pad_maximum_fusion.2
  145.4 1.4 copy.15
  146.8 1.8 reshape.43
  148.6 1.6 copy-done.1
  150.3 8.5 %pad_maximum_fusion.1 = bf16[16,3,64,1536]{3,2,1,0:T(8,128)(2,1)} fusion(bf16[16,1,64,1536]{3,2,1,0:T(8,128)(2,1)} %bitcast.11, bf16[16,1,64,1536]{3,2,1,0:T(8,128)(2,1)} %bitcast.32, bf16[16,1,64,1536]{3,2,1,0:T(8,128)(2,1)} %bitcast.31), kind=kLoop, calls=%fused_computation.22 | loop fusion | flops 9437184 | bytes 18874368 | tf_op jit(solution)/shard_map/stack | solution.py:44
  158.8 6.9 %pad_maximum_fusion = bf16[16,3,64,1536]{3,2,1,0:T(8,128)(2,1)} fusion(bf16[16,1,64,1536]{3,2,1,0:T(8,128)(2,1)} %bitcast.3, bf16[16,1,64,1536]{3,2,1,0:T(8,128)(2,1)} %bitcast.2, bf16[16,1,64,1536]{3,2,1,0:T(8,128)(2,1)S(1)} %bitcast.30), kind=kLoop, calls=%fused_computation.21 | loop fusion | flops 9437184 | bytes 18874368 | tf_op jit(solution)/shard_map/stack | solution.py:43
  166.4 70.5 %while.14 = (s32[]{:T(128)}, bf16[4,256,1536]{2,1,0:T(8,128)(2,1)S(1)}, bf16[256,1536]{1,0:T(8,128)(2,1)}, bf16[3072,1536]{1,0:T(8,128)(2,1)}, bf16[12,4,3072]{2...) while((s32[]{:T(128)}, ...), condition=%wide.region_6.7_spmd.clone, body=%wide.region_3.6_spmd.clone.sunk | while | flops 1016332032 | bytes 11436207 | solution.py:83
  166.4 2.2 fusion.32
  169.3 3.0 %fusion.34 = bf16[4,256,1536]{2,1,0:T(8,128)(2,1)S(1)} fusion(bf16[4,256,1536]{2,1,0:T(8,128)(2,1)S(1)} %get-tuple-element.255, s32[]{:T(128)S(6)} %select_n.41, bf16[4,3072]{1,0:T(4,128)(2,1)S(1)} %dynamic-slice_bitcast_fusion.2, bf16[256,3072]{1,0:T(8,128)(2,1)S(1)} %get-tuple-element.239, bf16[3072,1536]{1,0:T(8,128)(2,1)} %get-tuple-element.272, ...), kind=kOutput, calls=%fused_computation.12.clone.1 | convolution fusion | flops 808714240 | bytes 2648064 | tf_op jit(solution)/shard_map/while/body/eval_jaxpr/srk,kd->srd/dot_general | solution.py:78
  172.3 2.2 fusion.32
  175.1 3.0 %fusion.34 = bf16[4,256,1536]{2,1,0:T(8,128)(2,1)S(1)} fusion(bf16[4,256,1536]{2,1,0:T(8,128)(2,1)S(1)} %get-tuple-element.255, s32[]{:T(128)S(6)} %select_n.41, bf16[4,3072]{1,0:T(4,128)(2,1)S(1)} %dynamic-slice_bitcast_fusion.2, bf16[256,3072]{1,0:T(8,128)(2,1)S(1)} %get-tuple-element.239, bf16[3072,1536]{1,0:T(8,128)(2,1)} %get-tuple-element.272, ...), kind=kOutput, calls=%fused_computation.12.clone.1 | convolution fusion | flops 808714240 | bytes 2648064 | tf_op jit(solution)/shard_map/while/body/eval_jaxpr/srk,kd->srd/dot_general | solution.py:78
  178.2 2.2 fusion.32
  181.0 3.0 %fusion.34 = bf16[4,256,1536]{2,1,0:T(8,128)(2,1)S(1)} fusion(bf16[4,256,1536]{2,1,0:T(8,128)(2,1)S(1)} %get-tuple-element.255, s32[]{:T(128)S(6)} %select_n.41, bf16[4,3072]{1,0:T(4,128)(2,1)S(1)} %dynamic-slice_bitcast_fusion.2, bf16[256,3072]{1,0:T(8,128)(2,1)S(1)} %get-tuple-element.239, bf16[3072,1536]{1,0:T(8,128)(2,1)} %get-tuple-element.272, ...), kind=kOutput, calls=%fused_computation.12.clone.1 | convolution fusion | flops 808714240 | bytes 2648064 | tf_op jit(solution)/shard_map/while/body/eval_jaxpr/srk,kd->srd/dot_general | solution.py:78
  184.1 2.2 fusion.32
  186.9 3.0 %fusion.34 = bf16[4,256,1536]{2,1,0:T(8,128)(2,1)S(1)} fusion(bf16[4,256,1536]{2,1,0:T(8,128)(2,1)S(1)} %get-tuple-element.255, s32[]{:T(128)S(6)} %select_n.41, bf16[4,3072]{1,0:T(4,128)(2,1)S(1)} %dynamic-slice_bitcast_fusion.2, bf16[256,3072]{1,0:T(8,128)(2,1)S(1)} %get-tuple-element.239, bf16[3072,1536]{1,0:T(8,128)(2,1)} %get-tuple-element.272, ...), kind=kOutput, calls=%fused_computation.12.clone.1 | convolution fusion | flops 808714240 | bytes 2648064 | tf_op jit(solution)/shard_map/while/body/eval_jaxpr/srk,kd->srd/dot_general | solution.py:78
  189.9 2.2 fusion.32
  192.8 3.0 %fusion.34 = bf16[4,256,1536]{2,1,0:T(8,128)(2,1)S(1)} fusion(bf16[4,256,1536]{2,1,0:T(8,128)(2,1)S(1)} %get-tuple-element.255, s32[]{:T(128)S(6)} %select_n.41, bf16[4,3072]{1,0:T(4,128)(2,1)S(1)} %dynamic-slice_bitcast_fusion.2, bf16[256,3072]{1,0:T(8,128)(2,1)S(1)} %get-tuple-element.239, bf16[3072,1536]{1,0:T(8,128)(2,1)} %get-tuple-element.272, ...), kind=kOutput, calls=%fused_computation.12.clone.1 | convolution fusion | flops 808714240 | bytes 2648064 | tf_op jit(solution)/shard_map/while/body/eval_jaxpr/srk,kd->srd/dot_general | solution.py:78
  195.8 2.2 fusion.32
  198.6 3.0 %fusion.34 = bf16[4,256,1536]{2,1,0:T(8,128)(2,1)S(1)} fusion(bf16[4,256,1536]{2,1,0:T(8,128)(2,1)S(1)} %get-tuple-element.255, s32[]{:T(128)S(6)} %select_n.41, bf16[4,3072]{1,0:T(4,128)(2,1)S(1)} %dynamic-slice_bitcast_fusion.2, bf16[256,3072]{1,0:T(8,128)(2,1)S(1)} %get-tuple-element.239, bf16[3072,1536]{1,0:T(8,128)(2,1)} %get-tuple-element.272, ...), kind=kOutput, calls=%fused_computation.12.clone.1 | convolution fusion | flops 808714240 | bytes 2648064 | tf_op jit(solution)/shard_map/while/body/eval_jaxpr/srk,kd->srd/dot_general | solution.py:78
  201.7 2.2 fusion.32
  204.5 3.0 %fusion.34 = bf16[4,256,1536]{2,1,0:T(8,128)(2,1)S(1)} fusion(bf16[4,256,1536]{2,1,0:T(8,128)(2,1)S(1)} %get-tuple-element.255, s32[]{:T(128)S(6)} %select_n.41, bf16[4,3072]{1,0:T(4,128)(2,1)S(1)} %dynamic-slice_bitcast_fusion.2, bf16[256,3072]{1,0:T(8,128)(2,1)S(1)} %get-tuple-element.239, bf16[3072,1536]{1,0:T(8,128)(2,1)} %get-tuple-element.272, ...), kind=kOutput, calls=%fused_computation.12.clone.1 | convolution fusion | flops 808714240 | bytes 2648064 | tf_op jit(solution)/shard_map/while/body/eval_jaxpr/srk,kd->srd/dot_general | solution.py:78
  207.6 2.2 fusion.32
  210.4 3.0 %fusion.34 = bf16[4,256,1536]{2,1,0:T(8,128)(2,1)S(1)} fusion(bf16[4,256,1536]{2,1,0:T(8,128)(2,1)S(1)} %get-tuple-element.255, s32[]{:T(128)S(6)} %select_n.41, bf16[4,3072]{1,0:T(4,128)(2,1)S(1)} %dynamic-slice_bitcast_fusion.2, bf16[256,3072]{1,0:T(8,128)(2,1)S(1)} %get-tuple-element.239, bf16[3072,1536]{1,0:T(8,128)(2,1)} %get-tuple-element.272, ...), kind=kOutput, calls=%fused_computation.12.clone.1 | convolution fusion | flops 808714240 | bytes 2648064 | tf_op jit(solution)/shard_map/while/body/eval_jaxpr/srk,kd->srd/dot_general | solution.py:78
  213.5 2.2 fusion.32
  216.3 3.0 %fusion.34 = bf16[4,256,1536]{2,1,0:T(8,128)(2,1)S(1)} fusion(bf16[4,256,1536]{2,1,0:T(8,128)(2,1)S(1)} %get-tuple-element.255, s32[]{:T(128)S(6)} %select_n.41, bf16[4,3072]{1,0:T(4,128)(2,1)S(1)} %dynamic-slice_bitcast_fusion.2, bf16[256,3072]{1,0:T(8,128)(2,1)S(1)} %get-tuple-element.239, bf16[3072,1536]{1,0:T(8,128)(2,1)} %get-tuple-element.272, ...), kind=kOutput, calls=%fused_computation.12.clone.1 | convolution fusion | flops 808714240 | bytes 2648064 | tf_op jit(solution)/shard_map/while/body/eval_jaxpr/srk,kd->srd/dot_general | solution.py:78
  219.3 2.2 fusion.32
  222.2 3.0 %fusion.34 = bf16[4,256,1536]{2,1,0:T(8,128)(2,1)S(1)} fusion(bf16[4,256,1536]{2,1,0:T(8,128)(2,1)S(1)} %get-tuple-element.255, s32[]{:T(128)S(6)} %select_n.41, bf16[4,3072]{1,0:T(4,128)(2,1)S(1)} %dynamic-slice_bitcast_fusion.2, bf16[256,3072]{1,0:T(8,128)(2,1)S(1)} %get-tuple-element.239, bf16[3072,1536]{1,0:T(8,128)(2,1)} %get-tuple-element.272, ...), kind=kOutput, calls=%fused_computation.12.clone.1 | convolution fusion | flops 808714240 | bytes 2648064 | tf_op jit(solution)/shard_map/while/body/eval_jaxpr/srk,kd->srd/dot_general | solution.py:78
  225.2 2.2 fusion.32
  228.0 3.0 %fusion.34 = bf16[4,256,1536]{2,1,0:T(8,128)(2,1)S(1)} fusion(bf16[4,256,1536]{2,1,0:T(8,128)(2,1)S(1)} %get-tuple-element.255, s32[]{:T(128)S(6)} %select_n.41, bf16[4,3072]{1,0:T(4,128)(2,1)S(1)} %dynamic-slice_bitcast_fusion.2, bf16[256,3072]{1,0:T(8,128)(2,1)S(1)} %get-tuple-element.239, bf16[3072,1536]{1,0:T(8,128)(2,1)} %get-tuple-element.272, ...), kind=kOutput, calls=%fused_computation.12.clone.1 | convolution fusion | flops 808714240 | bytes 2648064 | tf_op jit(solution)/shard_map/while/body/eval_jaxpr/srk,kd->srd/dot_general | solution.py:78
  231.1 2.2 fusion.32
  233.9 3.0 %fusion.34 = bf16[4,256,1536]{2,1,0:T(8,128)(2,1)S(1)} fusion(bf16[4,256,1536]{2,1,0:T(8,128)(2,1)S(1)} %get-tuple-element.255, s32[]{:T(128)S(6)} %select_n.41, bf16[4,3072]{1,0:T(4,128)(2,1)S(1)} %dynamic-slice_bitcast_fusion.2, bf16[256,3072]{1,0:T(8,128)(2,1)S(1)} %get-tuple-element.239, bf16[3072,1536]{1,0:T(8,128)(2,1)} %get-tuple-element.272, ...), kind=kOutput, calls=%fused_computation.12.clone.1 | convolution fusion | flops 808714240 | bytes 2648064 | tf_op jit(solution)/shard_map/while/body/eval_jaxpr/srk,kd->srd/dot_general | solution.py:78
  237.0 1.7 copy-done.2
  (61 shorter events, 8.8 us)
Async XLA Ops:
  6.5 46.4 %all-gather.5.cloned.1.call-start = ((), (), s32[]{:S(2)}) async-start(), calls=%async_computation.1 | async-start | bytes 3932160 | tf_op jit(solution)/shard_map/all_gather | solution.py:28
  7.3 89.8 %all-gather.3.cloned.1.call-start = ((), (), s32[]{:S(2)}) async-start(), calls=%async_computation | async-start | bytes 3932160 | tf_op jit(solution)/shard_map/all_gather | solution.py:27
  52.9 95.6 %collective-permute-start.4 = (bf16[16,64,1536]{2,1,0:T(8,128)(2,1)}, bf16[16,64,1536]{2,1,0:T(8,128)(2,1)S(1)}, u32[]{:S(2)}, u32[]{:S(2)}) collective-permute-start(bf16[16,64,1536]{2,1,0:T(8,128)(2,1)} %all-gather.5.cloned.1.call-done), channel_id=1, source_target_pairs={{0,1},{1,2},{2,3},{3,4},{4,5},{5,6},{6,7},{7,8},{8,9},{9,10},{10,1... | collective-permute-start | bytes 9437192 | tf_op jit(solution)/shard_map/ppermute | solution.py:12
  56.2 92.5 %collective-permute-start.5 = (bf16[16,64,1536]{2,1,0:T(8,128)(2,1)}, bf16[16,64,1536]{2,1,0:T(8,128)(2,1)}, u32[]{:S(2)}, u32[]{:S(2)}) collective-permute-start(bf16[16,64,1536]{2,1,0:T(8,128)(2,1)} %all-gather.5.cloned.1.call-done), channel_id=1, source_target_pairs={{0,63},{1,0},{2,1},{3,2},{4,3},{5,4},{6,5},{7,6},{8,7},{9,8},{10,9... | collective-permute-start | bytes 9437192 | tf_op jit(solution)/shard_map/ppermute | solution.py:12
  97.0 61.8 %collective-permute-start = (bf16[16,64,1536]{2,1,0:T(8,128)(2,1)}, bf16[16,64,1536]{2,1,0:T(8,128)(2,1)}, u32[]{:S(2)}, u32[]{:S(2)}) collective-permute-start(bf16[16,64,1536]{2,1,0:T(8,128)(2,1)} %all-gather.3.cloned.1.call-done), channel_id=1, source_target_pairs={{0,1},{1,2},{2,3},{3,4},{4,5},{5,6},{6,7},{7,8},{8,9},{9,10},{10,1... | collective-permute-start | bytes 9437192 | tf_op jit(solution)/shard_map/ppermute | solution.py:12
  100.2 58.5 %collective-permute-start.1 = (bf16[16,64,1536]{2,1,0:T(8,128)(2,1)}, bf16[16,64,1536]{2,1,0:T(8,128)(2,1)}, u32[]{:S(2)}, u32[]{:S(2)}) collective-permute-start(bf16[16,64,1536]{2,1,0:T(8,128)(2,1)} %all-gather.3.cloned.1.call-done), channel_id=1, source_target_pairs={{0,63},{1,0},{2,1},{3,2},{4,3},{5,4},{6,5},{7,6},{8,7},{9,8},{10,9... | collective-permute-start | bytes 9437192 | tf_op jit(solution)/shard_map/ppermute | solution.py:12
  110.8 26.0 %collective-permute-start.2 = (bf16[4,16,64,12]{2,0,3,1:T(4,128)(2,1)S(1)}, bf16[4,16,64,12]{2,0,3,1:T(4,128)(2,1)S(1)}, u32[]{:S(2)}, u32[]{:S(2)}) collective-permute-start(bf16[4,16,64,12]{2,0,3,1:T(4,128)(2,1)S(1)} %all_gather.10), channel_id=1, source_target_pairs={{0,1},{1,2},{2,3},{3,4},{4,5},{5,6},{6,7},{7,8},{8,9},{9,10},{10,1... | collective-permute-start | bytes 294920 | tf_op jit(solution)/shard_map/ppermute | solution.py:12
  136.8 7.1 %collective-permute-start.3 = (bf16[4,16,64,12]{2,0,3,1:T(4,128)(2,1)S(1)}, bf16[4,16,64,12]{2,0,3,1:T(4,128)(2,1)}, u32[]{:S(2)}, u32[]{:S(2)}) collective-permute-start(bf16[4,16,64,12]{2,0,3,1:T(4,128)(2,1)S(1)} %all_gather.10), channel_id=1, source_target_pairs={{0,63},{1,0},{2,1},{3,2},{4,3},{5,4},{6,5},{7,6},{8,7},{9,8},{10,9... | collective-permute-start | bytes 294920 | tf_op jit(solution)/shard_map/ppermute | solution.py:12
  148.6 1.7 copy-start.1
  150.3 8.5 %copy-start = (bf16[16,64,1536]{2,1,0:T(8,128)(2,1)S(1)}, bf16[16,64,1536]{2,1,0:T(8,128)(2,1)}, u32[]{:S(2)}) copy-start(bf16[16,64,1536]{2,1,0:T(8,128)(2,1)} %all-gather.3.cloned.1.call-done) | copy-start | bytes 9437188
  165.7 0.7 copy-start.3
  165.7 0.7 copy-start.4
  165.7 0.7 copy-start.5
  237.0 1.7 copy-start.2
Sparse Core Ops, SparseCore 0:
  9.1 43.7 all-gather.4
  54.8 42.2 all-gather.2
where the time goes:
time: 247 us; the launch traced here: 245 us
  waiting for transfers between devices  109 us (44%)
  matrix products  62.3 us (25%)
  other arithmetic  28.8 us (12%)
  between operations  13.5 us (5%)
  starting transfers between devices  12.1 us (5%)
  blocking collectives  9.6 us (4%)
  local copies, waits for them, and re-layouts  9.6 us (4%)
    all_gather x1, waiting for transfers between devices, per_device(): lax.all_gather(value_rows, 'tm', axis=0, tiled=True)  44.9 us
    all_gather x1, waiting for transfers between devices, per_device(): lax.all_gather(key_rows, 'tm', axis=0, tiled=True)  40.9 us
    dot_general x12, matrix products, one_head(): jnp.einsum('srk,kd->srd', dropped, value_h, preferred_element_type=jnp.fl...  36.4 us
    dot_general x12, matrix products, one_head(): jnp.einsum('rd,kd->rk', query_h, key_h, preferred_element_type=jnp.float32)  26 us
    ppermute x6, waiting for transfers between devices, from_behind(): lax.ppermute(shard, axis, [(i, (i + by) % peers) for i in range(peers)])  21.9 us
    ppermute x6, starting transfers between devices, from_behind(): lax.ppermute(shard, axis, [(i, (i + by) % peers) for i in range(peers)])  12 us
    all_gather x1, blocking collectives, per_device(): lax.all_gather(drop_low, 'tm', axis=1, tiled=True)  9.6 us
    another operation x1, other arithmetic, per_device(): window_values = jnp.stack(value_parts, axis=1)  8.52 us
  transfers between devices with their start and end apart: 8, of which 4 were waited for; matrix products, arithmetic and copies ran while one was open for 8% of the time, Pallas kernels for 0%

commit v1 on v0

--- a/solution.py
+++ b/solution.py
@@ -25,7 +25,9 @@
     drop_low = dropout.astype(jnp.bfloat16)
     all_keys, all_values, all_drops = (
         lax.all_gather(key_rows, "tm", axis=0, tiled=True),
-        lax.all_gather(value_rows, "tm", axis=0, tiled=True),
+        jnp.concatenate(
+            lax.all_to_all(jnp.stack([value_rows] * lax.axis_size("tm")), "tm", 0, 0), axis=0
+        ),
         lax.all_gather(drop_low, "tm", axis=1, tiled=True),
     )
     key_parts = [all_keys]

time: 247 us -> 257 us (1.040)
  blocking collectives: 9.6 us -> 71.6 us
  waiting for transfers between devices: 109 us -> 55 us
  starting transfers between devices: 12.1 us -> 16.5 us
    all_to_all x0 -> x1, blocking collectives: none -> 62.3 us  [per_device(): lax.all_to_all(jnp.stack([value_rows] * lax.axis_size('tm')), 'tm', 0, 0)]
    all_gather x1 -> x0, waiting for transfers between devices: 44.9 us -> none  [per_device(): lax.all_gather(value_rows, 'tm', axis=0, tiled=True)]
    all_gather x1, waiting for transfers between devices: 40.9 us -> 0.01 us  [per_device(): lax.all_gather(key_rows, 'tm', axis=0, tiled=True)]
    ppermute x6, waiting for transfers between devices: 21.9 us -> 54.3 us  [from_behind(): lax.ppermute(shard, axis, [(i, (i + by) % peers) for i in range(peers)])]
    ppermute x6, starting transfers between devices: 12 us -> 16.5 us  [from_behind(): lax.ppermute(shard, axis, [(i, (i + by) % peers) for i in range(peers)])]
  transfers between devices with their start and end apart: 8 -> 7, of which waited for: 4 -> 2; matrix products, arithmetic and copies ran while one was open for 8% -> 7% of each run, Pallas kernels for 0% -> 0%
where the time goes in v1:
time: 257 us; the launch traced here: 256 us
  blocking collectives  71.6 us (28%)
  matrix products  62.4 us (24%)
  waiting for transfers between devices  55 us (21%)
  other arithmetic  27.1 us (11%)
  starting transfers between devices  16.5 us (6%)
  between operations  13.5 us (5%)
  local copies, waits for them, and re-layouts  9.35 us (4%)
    all_to_all x1, blocking collectives, per_device(): lax.all_to_all(jnp.stack([value_rows] * lax.axis_size('tm')), 'tm', 0, 0)  62.3 us
    ppermute x6, waiting for transfers between devices, from_behind(): lax.ppermute(shard, axis, [(i, (i + by) % peers) for i in range(peers)])  54.3 us
    dot_general x12, matrix products, one_head(): jnp.einsum('srk,kd->srd', dropped, value_h, preferred_element_type=jnp.fl...  36.4 us
    dot_general x12, matrix products, one_head(): jnp.einsum('rd,kd->rk', query_h, key_h, preferred_element_type=jnp.float32)  26 us
    ppermute x6, starting transfers between devices, from_behind(): lax.ppermute(shard, axis, [(i, (i + by) % peers) for i in range(peers)])  16.5 us
    all_gather x1, blocking collectives, per_device(): lax.all_gather(drop_low, 'tm', axis=1, tiled=True)  9.31 us
    another operation x1, other arithmetic, per_device(): window_keys = jnp.stack(key_parts, axis=1)  8.4 us
    reduce_sum x12, other arithmetic, one_head(): total = jnp.sum(weight, axis=1)  7.42 us
  transfers between devices with their start and end apart: 7, of which 2 were waited for; matrix products, arithmetic and copies ran while one was open for 7% of the time, Pallas kernels for 0%

profile of v1, /device:TPU:97, one launch (start us, length us, event | category | flops | bytes accessed | tf_op | source)
XLA Modules:
  0.0 255.7 jit_solution(6274534782779789237)
XLA Ops:
  6.5 0.7 all-gather.2.cloned.1.call-update
  7.3 1.4 stack.64
  8.7 62.3 %all_to_all.5 = bf16[4,4,64,1536]{3,2,1,0:T(8,128)(2,1)S(1)} all-to-all(bf16[4,4,64,1536]{3,2,1,0:T(8,128)(2,1)S(1)} %stack.64), channel_id=1, replica_groups=mesh['tm'=4,'space'=64] {'tm'}, dimensions={0} | all-to-all | bytes 6291456 | tf_op jit(solution)/shard_map/all_to_all | solution.py:29
  71.0 7.7 %collective-permute-start.4 = (bf16[16,64,1536]{2,1,0:T(8,128)(2,1)S(1)}, bf16[16,64,1536]{2,1,0:T(8,128)(2,1)}, u32[]{:S(2)}, u32[]{:S(2)}) collective-permute-start(bf16[16,64,1536]{2,1,0:T(8,128)(2,1)S(1)} %bitcast.31), channel_id=1, source_target_pairs={{0,1},{1,2},{2,3},{3,4},{4,5},{5,6},{6,7},{7,8},{8,9},{9,10},{10,1... | collective-permute-start | bytes 9437192 | tf_op jit(solution)/shard_map/ppermute | solution.py:12
  78.8 3.0 %collective-permute-start = (bf16[16,64,1536]{2,1,0:T(8,128)(2,1)}, bf16[16,64,1536]{2,1,0:T(8,128)(2,1)}, u32[]{:S(2)}, u32[]{:S(2)}) collective-permute-start(bf16[16,64,1536]{2,1,0:T(8,128)(2,1)} %all-gather.2.cloned.1.call-done), channel_id=1, source_target_pairs={{0,1},{1,2},{2,3},{3,4},{4,5},{5,6},{6,7},{7,8},{8,9},{9,10},{10,1... | collective-permute-start | bytes 9437192 | tf_op jit(solution)/shard_map/ppermute | solution.py:12
  81.8 9.3 %all_gather.7 = bf16[4,16,64,12]{2,0,3,1:T(4,128)(2,1)S(1)} all-gather(bf16[4,4,64,12]{2,0,3,1:T(4,128)(2,1)S(1)} %copy_convert_fusion), channel_id=1, replica_groups=mesh['tm'=4,'space'=64] {'tm'}, dimensions={1}, use_global_device_ids=true | all-gather | bytes 122880 | tf_op jit(solution)/shard_map/all_gather | solution.py:31
  91.1 5.8 %collective-permute-start.2 = (bf16[4,16,64,12]{2,0,3,1:T(4,128)(2,1)S(1)}, bf16[4,16,64,12]{2,0,3,1:T(4,128)(2,1)S(1)}, u32[]{:S(2)}, u32[]{:S(2)}) collective-permute-start(bf16[4,16,64,12]{2,0,3,1:T(4,128)(2,1)S(1)} %all_gather.7), channel_id=1, source_target_pairs={{0,1},{1,2},{2,3},{3,4},{4,5},{5,6},{6,7},{7,8},{8,9},{9,10},{10,1... | collective-permute-start | bytes 294920 | tf_op jit(solution)/shard_map/ppermute | solution.py:12
  96.8 0.7 compare_reduce_fusion.2
  97.5 2.0 pad_add_fusion
  99.7 0.7 and.23
  100.4 48.4 %collective-permute-done.2 = bf16[4,16,64,12]{2,0,3,1:T(4,128)(2,1)S(1)} collective-permute-done((bf16[4,16,64,12]{2,0,3,1:T(4,128)(2,1)S(1)}, bf16[4,16,64,12]{2,0,3,1:T(4,128)(2,1)S(1)}, u32[]{:S(2)}, u32[]{:S(2)}) %collective-permute-start.2) | collective-permute-done | bytes 98336 | tf_op jit(solution)/shard_map/ppermute | solution.py:12
  149.4 0.7 le.15
  150.1 5.8 %collective-permute-done.3 = bf16[4,16,64,12]{2,0,3,1:T(4,128)(2,1)} collective-permute-done((bf16[4,16,64,12]{2,0,3,1:T(4,128)(2,1)S(1)}, bf16[4,16,64,12]{2,0,3,1:T(4,128)(2,1)}, u32[]{:S(2)}, u32[]{:S(2)}) %collective-permute-start.3) | collective-permute-done | bytes 98336 | tf_op jit(solution)/shard_map/ppermute | solution.py:12
  155.9 1.5 pad_maximum_fusion.2
  157.4 1.4 copy.16
  158.8 1.8 reshape.48
  160.6 7.0 %pad_maximum_fusion.1 = bf16[16,3,64,1536]{3,2,1,0:T(8,128)(2,1)} fusion(bf16[16,1,64,1536]{3,2,1,0:T(8,128)(2,1)} %bitcast.13, bf16[16,1,64,1536]{3,2,1,0:T(8,128)(2,1)} %bitcast.12, bf16[16,1,64,1536]{3,2,1,0:T(8,128)(2,1)S(1)} %bitcast.33), kind=kLoop, calls=%fused_computation.22 | loop fusion | flops 9437184 | bytes 18874368 | tf_op jit(solution)/shard_map/stack | solution.py:46
  167.6 8.4 %pad_maximum_fusion = bf16[16,3,64,1536]{3,2,1,0:T(8,128)(2,1)} fusion(bf16[16,1,64,1536]{3,2,1,0:T(8,128)(2,1)} %bitcast.3, bf16[16,1,64,1536]{3,2,1,0:T(8,128)(2,1)} %bitcast.2, bf16[16,1,64,1536]{3,2,1,0:T(8,128)(2,1)} %bitcast.36), kind=kLoop, calls=%fused_computation.21 | loop fusion | flops 9437184 | bytes 18874368 | tf_op jit(solution)/shard_map/stack | solution.py:45
  176.7 70.5 %while.14 = (s32[]{:T(128)}, bf16[4,256,1536]{2,1,0:T(8,128)(2,1)S(1)}, bf16[256,1536]{1,0:T(8,128)(2,1)}, bf16[3072,1536]{1,0:T(8,128)(2,1)}, bf16[12,4,3072]{2...) while((s32[]{:T(128)}, ...), condition=%wide.region_6.7_spmd.clone, body=%wide.region_3.6_spmd.clone.sunk | while | flops 1016332032 | bytes 11436207 | solution.py:85
  176.7 2.2 fusion.32
  178.9 0.6 fusion.33
  179.5 3.0 %fusion.34 = bf16[4,256,1536]{2,1,0:T(8,128)(2,1)S(1)} fusion(bf16[4,256,1536]{2,1,0:T(8,128)(2,1)S(1)} %get-tuple-element.255, s32[]{:T(128)S(6)} %select_n.41, bf16[4,3072]{1,0:T(4,128)(2,1)S(1)} %dynamic-slice_bitcast_fusion.2, bf16[256,3072]{1,0:T(8,128)(2,1)S(1)} %get-tuple-element.239, bf16[3072,1536]{1,0:T(8,128)(2,1)} %get-tuple-element.272, ...), kind=kOutput, calls=%fused_computation.12.clone.1 | convolution fusion | flops 808714240 | bytes 2648064 | tf_op jit(solution)/shard_map/while/body/eval_jaxpr/srk,kd->srd/dot_general | solution.py:80
  182.6 2.2 fusion.32
  184.7 0.6 fusion.33
  185.4 3.0 %fusion.34 = bf16[4,256,1536]{2,1,0:T(8,128)(2,1)S(1)} fusion(bf16[4,256,1536]{2,1,0:T(8,128)(2,1)S(1)} %get-tuple-element.255, s32[]{:T(128)S(6)} %select_n.41, bf16[4,3072]{1,0:T(4,128)(2,1)S(1)} %dynamic-slice_bitcast_fusion.2, bf16[256,3072]{1,0:T(8,128)(2,1)S(1)} %get-tuple-element.239, bf16[3072,1536]{1,0:T(8,128)(2,1)} %get-tuple-element.272, ...), kind=kOutput, calls=%fused_computation.12.clone.1 | convolution fusion | flops 808714240 | bytes 2648064 | tf_op jit(solution)/shard_map/while/body/eval_jaxpr/srk,kd->srd/dot_general | solution.py:80
  188.4 2.2 fusion.32
  190.6 0.6 fusion.33
  191.3 3.0 %fusion.34 = bf16[4,256,1536]{2,1,0:T(8,128)(2,1)S(1)} fusion(bf16[4,256,1536]{2,1,0:T(8,128)(2,1)S(1)} %get-tuple-element.255, s32[]{:T(128)S(6)} %select_n.41, bf16[4,3072]{1,0:T(4,128)(2,1)S(1)} %dynamic-slice_bitcast_fusion.2, bf16[256,3072]{1,0:T(8,128)(2,1)S(1)} %get-tuple-element.239, bf16[3072,1536]{1,0:T(8,128)(2,1)} %get-tuple-element.272, ...), kind=kOutput, calls=%fused_computation.12.clone.1 | convolution fusion | flops 808714240 | bytes 2648064 | tf_op jit(solution)/shard_map/while/body/eval_jaxpr/srk,kd->srd/dot_general | solution.py:80
  194.3 2.2 fusion.32
  197.1 3.0 %fusion.34 = bf16[4,256,1536]{2,1,0:T(8,128)(2,1)S(1)} fusion(bf16[4,256,1536]{2,1,0:T(8,128)(2,1)S(1)} %get-tuple-element.255, s32[]{:T(128)S(6)} %select_n.41, bf16[4,3072]{1,0:T(4,128)(2,1)S(1)} %dynamic-slice_bitcast_fusion.2, bf16[256,3072]{1,0:T(8,128)(2,1)S(1)} %get-tuple-element.239, bf16[3072,1536]{1,0:T(8,128)(2,1)} %get-tuple-element.272, ...), kind=kOutput, calls=%fused_computation.12.clone.1 | convolution fusion | flops 808714240 | bytes 2648064 | tf_op jit(solution)/shard_map/while/body/eval_jaxpr/srk,kd->srd/dot_general | solution.py:80
  200.2 2.2 fusion.32
  203.0 3.0 %fusion.34 = bf16[4,256,1536]{2,1,0:T(8,128)(2,1)S(1)} fusion(bf16[4,256,1536]{2,1,0:T(8,128)(2,1)S(1)} %get-tuple-element.255, s32[]{:T(128)S(6)} %select_n.41, bf16[4,3072]{1,0:T(4,128)(2,1)S(1)} %dynamic-slice_bitcast_fusion.2, bf16[256,3072]{1,0:T(8,128)(2,1)S(1)} %get-tuple-element.239, bf16[3072,1536]{1,0:T(8,128)(2,1)} %get-tuple-element.272, ...), kind=kOutput, calls=%fused_computation.12.clone.1 | convolution fusion | flops 808714240 | bytes 2648064 | tf_op jit(solution)/shard_map/while/body/eval_jaxpr/srk,kd->srd/dot_general | solution.py:80
  206.1 2.2 fusion.32
  208.2 0.6 fusion.33
  208.9 3.0 %fusion.34 = bf16[4,256,1536]{2,1,0:T(8,128)(2,1)S(1)} fusion(bf16[4,256,1536]{2,1,0:T(8,128)(2,1)S(1)} %get-tuple-element.255, s32[]{:T(128)S(6)} %select_n.41, bf16[4,3072]{1,0:T(4,128)(2,1)S(1)} %dynamic-slice_bitcast_fusion.2, bf16[256,3072]{1,0:T(8,128)(2,1)S(1)} %get-tuple-element.239, bf16[3072,1536]{1,0:T(8,128)(2,1)} %get-tuple-element.272, ...), kind=kOutput, calls=%fused_computation.12.clone.1 | convolution fusion | flops 808714240 | bytes 2648064 | tf_op jit(solution)/shard_map/while/body/eval_jaxpr/srk,kd->srd/dot_general | solution.py:80
  212.0 2.2 fusion.32
  214.8 3.0 %fusion.34 = bf16[4,256,1536]{2,1,0:T(8,128)(2,1)S(1)} fusion(bf16[4,256,1536]{2,1,0:T(8,128)(2,1)S(1)} %get-tuple-element.255, s32[]{:T(128)S(6)} %select_n.41, bf16[4,3072]{1,0:T(4,128)(2,1)S(1)} %dynamic-slice_bitcast_fusion.2, bf16[256,3072]{1,0:T(8,128)(2,1)S(1)} %get-tuple-element.239, bf16[3072,1536]{1,0:T(8,128)(2,1)} %get-tuple-element.272, ...), kind=kOutput, calls=%fused_computation.12.clone.1 | convolution fusion | flops 808714240 | bytes 2648064 | tf_op jit(solution)/shard_map/while/body/eval_jaxpr/srk,kd->srd/dot_general | solution.py:80
  217.8 2.2 fusion.32
  220.7 3.0 %fusion.34 = bf16[4,256,1536]{2,1,0:T(8,128)(2,1)S(1)} fusion(bf16[4,256,1536]{2,1,0:T(8,128)(2,1)S(1)} %get-tuple-element.255, s32[]{:T(128)S(6)} %select_n.41, bf16[4,3072]{1,0:T(4,128)(2,1)S(1)} %dynamic-slice_bitcast_fusion.2, bf16[256,3072]{1,0:T(8,128)(2,1)S(1)} %get-tuple-element.239, bf16[3072,1536]{1,0:T(8,128)(2,1)} %get-tuple-element.272, ...), kind=kOutput, calls=%fused_computation.12.clone.1 | convolution fusion | flops 808714240 | bytes 2648064 | tf_op jit(solution)/shard_map/while/body/eval_jaxpr/srk,kd->srd/dot_general | solution.py:80
  223.7 2.2 fusion.32
  226.5 3.0 %fusion.34 = bf16[4,256,1536]{2,1,0:T(8,128)(2,1)S(1)} fusion(bf16[4,256,1536]{2,1,0:T(8,128)(2,1)S(1)} %get-tuple-element.255, s32[]{:T(128)S(6)} %select_n.41, bf16[4,3072]{1,0:T(4,128)(2,1)S(1)} %dynamic-slice_bitcast_fusion.2, bf16[256,3072]{1,0:T(8,128)(2,1)S(1)} %get-tuple-element.239, bf16[3072,1536]{1,0:T(8,128)(2,1)} %get-tuple-element.272, ...), kind=kOutput, calls=%fused_computation.12.clone.1 | convolution fusion | flops 808714240 | bytes 2648064 | tf_op jit(solution)/shard_map/while/body/eval_jaxpr/srk,kd->srd/dot_general | solution.py:80
  229.6 2.2 fusion.32
  232.4 3.0 %fusion.34 = bf16[4,256,1536]{2,1,0:T(8,128)(2,1)S(1)} fusion(bf16[4,256,1536]{2,1,0:T(8,128)(2,1)S(1)} %get-tuple-element.255, s32[]{:T(128)S(6)} %select_n.41, bf16[4,3072]{1,0:T(4,128)(2,1)S(1)} %dynamic-slice_bitcast_fusion.2, bf16[256,3072]{1,0:T(8,128)(2,1)S(1)} %get-tuple-element.239, bf16[3072,1536]{1,0:T(8,128)(2,1)} %get-tuple-element.272, ...), kind=kOutput, calls=%fused_computation.12.clone.1 | convolution fusion | flops 808714240 | bytes 2648064 | tf_op jit(solution)/shard_map/while/body/eval_jaxpr/srk,kd->srd/dot_general | solution.py:80
  235.5 2.2 fusion.32
  238.3 3.0 %fusion.34 = bf16[4,256,1536]{2,1,0:T(8,128)(2,1)S(1)} fusion(bf16[4,256,1536]{2,1,0:T(8,128)(2,1)S(1)} %get-tuple-element.255, s32[]{:T(128)S(6)} %select_n.41, bf16[4,3072]{1,0:T(4,128)(2,1)S(1)} %dynamic-slice_bitcast_fusion.2, bf16[256,3072]{1,0:T(8,128)(2,1)S(1)} %get-tuple-element.239, bf16[3072,1536]{1,0:T(8,128)(2,1)} %get-tuple-element.272, ...), kind=kOutput, calls=%fused_computation.12.clone.1 | convolution fusion | flops 808714240 | bytes 2648064 | tf_op jit(solution)/shard_map/while/body/eval_jaxpr/srk,kd->srd/dot_general | solution.py:80
  241.3 2.2 fusion.32
  244.2 3.0 %fusion.34 = bf16[4,256,1536]{2,1,0:T(8,128)(2,1)S(1)} fusion(bf16[4,256,1536]{2,1,0:T(8,128)(2,1)S(1)} %get-tuple-element.255, s32[]{:T(128)S(6)} %select_n.41, bf16[4,3072]{1,0:T(4,128)(2,1)S(1)} %dynamic-slice_bitcast_fusion.2, bf16[256,3072]{1,0:T(8,128)(2,1)S(1)} %get-tuple-element.239, bf16[3072,1536]{1,0:T(8,128)(2,1)} %get-tuple-element.272, ...), kind=kOutput, calls=%fused_computation.12.clone.1 | convolution fusion | flops 808714240 | bytes 2648064 | tf_op jit(solution)/shard_map/while/body/eval_jaxpr/srk,kd->srd/dot_general | solution.py:80
  247.2 1.7 copy-done
  (60 shorter events, 6.8 us)
Async XLA Ops:
  6.5 72.2 %all-gather.2.cloned.1.call-start = ((), (), s32[]{:S(2)}) async-start(), calls=%async_computation.1 | async-start | bytes 3932160 | tf_op jit(solution)/shard_map/all_gather | solution.py:27
  8.7 73.0 %copy-start.1 = (s32[4,4,64,12]{2,1,3,0:T(4,128)S(1)}, s32[4,4,64,12]{2,1,3,0:T(4,128)}, u32[]{:S(2)}) copy-start(s32[4,4,64,12]{2,1,3,0:T(4,128)} %param.10) | copy-start | bytes 147460
  8.7 88.1 %copy-start.5 = (s32[1,2]{1,0:T(1,128)S(1)}, s32[1,2]{1,0:T(1,128)}, u32[]{:S(2)}) copy-start(s32[1,2]{1,0:T(1,128)} %param.11) | copy-start | bytes 28
  71.0 89.6 %collective-permute-start.4 = (bf16[16,64,1536]{2,1,0:T(8,128)(2,1)S(1)}, bf16[16,64,1536]{2,1,0:T(8,128)(2,1)}, u32[]{:S(2)}, u32[]{:S(2)}) collective-permute-start(bf16[16,64,1536]{2,1,0:T(8,128)(2,1)S(1)} %bitcast.31), channel_id=1, source_target_pairs={{0,1},{1,2},{2,3},{3,4},{4,5},{5,6},{6,7},{7,8},{8,9},{9,10},{10,1... | collective-permute-start | bytes 9437192 | tf_op jit(solution)/shard_map/ppermute | solution.py:12
  78.8 81.8 %collective-permute-start.5 = (bf16[16,64,1536]{2,1,0:T(8,128)(2,1)S(1)}, bf16[16,64,1536]{2,1,0:T(8,128)(2,1)}, u32[]{:S(2)}, u32[]{:S(2)}) collective-permute-start(bf16[16,64,1536]{2,1,0:T(8,128)(2,1)S(1)} %bitcast.32), channel_id=1, source_target_pairs={{0,63},{1,0},{2,1},{3,2},{4,3},{5,4},{6,5},{7,6},{8,7},{9,8},{10,9... | collective-permute-start | bytes 9437192 | tf_op jit(solution)/shard_map/ppermute | solution.py:12
  78.8 88.8 %collective-permute-start = (bf16[16,64,1536]{2,1,0:T(8,128)(2,1)}, bf16[16,64,1536]{2,1,0:T(8,128)(2,1)}, u32[]{:S(2)}, u32[]{:S(2)}) collective-permute-start(bf16[16,64,1536]{2,1,0:T(8,128)(2,1)} %all-gather.2.cloned.1.call-done), channel_id=1, source_target_pairs={{0,1},{1,2},{2,3},{3,4},{4,5},{5,6},{6,7},{7,8},{8,9},{9,10},{10,1... | collective-permute-start | bytes 9437192 | tf_op jit(solution)/shard_map/ppermute | solution.py:12
  81.7 85.9 %collective-permute-start.1 = (bf16[16,64,1536]{2,1,0:T(8,128)(2,1)}, bf16[16,64,1536]{2,1,0:T(8,128)(2,1)}, u32[]{:S(2)}, u32[]{:S(2)}) collective-permute-start(bf16[16,64,1536]{2,1,0:T(8,128)(2,1)} %all-gather.2.cloned.1.call-done), channel_id=1, source_target_pairs={{0,63},{1,0},{2,1},{3,2},{4,3},{5,4},{6,5},{7,6},{8,7},{9,8},{10,9... | collective-permute-start | bytes 9437192 | tf_op jit(solution)/shard_map/ppermute | solution.py:12
  91.1 57.7 %collective-permute-start.2 = (bf16[4,16,64,12]{2,0,3,1:T(4,128)(2,1)S(1)}, bf16[4,16,64,12]{2,0,3,1:T(4,128)(2,1)S(1)}, u32[]{:S(2)}, u32[]{:S(2)}) collective-permute-start(bf16[4,16,64,12]{2,0,3,1:T(4,128)(2,1)S(1)} %all_gather.7), channel_id=1, source_target_pairs={{0,1},{1,2},{2,3},{3,4},{4,5},{5,6},{6,7},{7,8},{8,9},{9,10},{10,1... | collective-permute-start | bytes 294920 | tf_op jit(solution)/shard_map/ppermute | solution.py:12
  148.8 7.1 %collective-permute-start.3 = (bf16[4,16,64,12]{2,0,3,1:T(4,128)(2,1)S(1)}, bf16[4,16,64,12]{2,0,3,1:T(4,128)(2,1)}, u32[]{:S(2)}, u32[]{:S(2)}) collective-permute-start(bf16[4,16,64,12]{2,0,3,1:T(4,128)(2,1)S(1)} %all_gather.7), channel_id=1, source_target_pairs={{0,63},{1,0},{2,1},{3,2},{4,3},{5,4},{6,5},{7,6},{8,7},{9,8},{10,9... | collective-permute-start | bytes 294920 | tf_op jit(solution)/shard_map/ppermute | solution.py:12
  176.0 0.7 copy-start.2
  176.0 0.7 copy-start.3
  176.0 0.7 copy-start.4
  247.2 1.7 copy-start
Sparse Core Ops, SparseCore 0:
  9.1 67.0 all-gather.1
